TPU v7x, 256 devices: a whole 4x4x8 slice. The times are simulated.
256 devices in a mesh: sect: 8 (over y, core), dir: 32 (over z, x).
Axes of the slice: x: 4, y: 4, z: 8, core: 2. Of those that a mesh axis runs over, the one named last changes fastest.
Arguments:
- unknowns: bfloat16 [2, 16, 64, 128, 256], P(None, 'sect', 'dir'), may hold values from -6 to 6
- leaf_live: int32 [16, 64], P('sect', 'dir'), may hold values from 0 to 1, as said below
- near_blocks: bfloat16 [2, 16, 64, 9, 128, 128], P(None, 'sect', 'dir'), may hold values from -0.125 to 0.125
- aggregate: bfloat16 [2, 16, 64, 512, 128], P(None, 'sect', 'dir'), may hold values from -0.1875 to 0.1875
- disaggregate: bfloat16 [2, 16, 64, 128, 512], P(None, 'sect', 'dir'), may hold values from -0.1875 to 0.1875
- translate: float32 [16, 2, 512], P(None, None, 'dir'), may hold values from -1.2 to 1.2
Outputs:
- field: float32 [2, 16, 64, 128, 256], P(None, 'sect', 'dir')
Inputs may be any that keep to these rules, and one draw needn't show every extreme that they name: `leaf_live`: every 2 x 2 block of leaves (one coarse box) has its first leaf live; in every draw some box has all four leaves live.
All inputs are finite; a program needn't handle non-finite values.
Results may differ from a plain program's by a relative error of at most 0.0036.
Values may be sent and summed in bfloat16 or wider, within the bound.
A program may use at most 64 MiB of HBM per device.

v0:
```python
import jax
import jax.numpy as jnp
from jax import lax
from jax.sharding import PartitionSpec as P

far_offsets = [
    (row_step, col_step)
    for row_step in range(-2, 3)
    for col_step in range(-2, 3)
    if max(abs(row_step), abs(col_step)) == 2
]


def with_halo(cells, sides, width):
    for axis, dim in sides:
        count = lax.axis_size(axis)
        ends = count - 1
        head = lax.slice_in_dim(cells, 0, width, axis=dim)
        tail = lax.slice_in_dim(cells, cells.shape[dim] - width, cells.shape[dim], axis=dim)
        cells = jnp.concatenate(
            [
                lax.ppermute(tail, axis, [(i, (i + 1) % count) for i in range(ends)]),
                cells,
                lax.ppermute(head, axis, [((i + 1) % count, i) for i in range(ends)]),
            ],
            axis=dim,
        )
    return cells


def cut_along(value, dim, devices):
    before, after = (value.shape[:dim], value.shape[dim + 1 :])
    return jnp.moveaxis(value.reshape(*before, devices, -1, *after), dim, 0)


def in_order(tiles, dim):
    tiles = jnp.moveaxis(tiles, 0, dim)
    dims = tiles.shape
    return tiles.reshape(*dims[:dim], dims[dim] * dims[dim + 1], *dims[dim + 2 :])


def joined_exchange(value, axis, axes, splits, concats):
    sizes = [lax.axis_size(a) for a in axes]
    tiles = cut_along(value, splits[0], sizes[0])
    tiles = jnp.moveaxis(cut_along(tiles, splits[1] + 1, sizes[1]), 0, 1)
    inside = tiles.shape[2:]
    tiles = tiles.reshape(-1, *inside)
    tiles = lax.all_to_all(tiles, axis, split_axis=0, concat_axis=0, tiled=True)
    tiles = in_order(tiles.reshape(*sizes, *inside), concats[0] + 1)
    return in_order(tiles, concats[1])


def complex_product(form, left, right):
    real = jnp.einsum(form, left[0], right[0], preferred_element_type=jnp.float32) - jnp.einsum(
        form, left[1], right[1], preferred_element_type=jnp.float32
    )
    imag = jnp.einsum(form, left[0], right[1], preferred_element_type=jnp.float32) + jnp.einsum(
        form, left[1], right[0], preferred_element_type=jnp.float32
    )
    return jnp.stack([real, imag])


def translate_grid(sources, coefs):
    box_rows = sources.shape[0]
    box_cols = sources.shape[1]
    widened = jnp.pad(sources.astype(jnp.float32), ((2, 2), (2, 2), (0, 0), (0, 0), (0, 0)))
    accum = jnp.zeros(sources.shape, jnp.float32)
    for row_step in range(-2, 3):
        total = jnp.zeros(sources.shape, jnp.float32)
        for index, (step_row, step_col) in enumerate(far_offsets):
            if step_row == row_step:
                shifted = widened[
                    2 + step_row : 2 + step_row + box_rows, 2 + step_col : 2 + step_col + box_cols
                ]
                coef_real = coefs[index, 0][None, None, :, None]
                coef_imag = coefs[index, 1][None, None, :, None]
                real = coef_real * shifted[:, :, 0] - coef_imag * shifted[:, :, 1]
                imag = coef_real * shifted[:, :, 1] + coef_imag * shifted[:, :, 0]
                total = total + jnp.stack([real, imag], axis=2)
        rounded = lax.optimization_barrier(total.astype(jnp.bfloat16))
        accum = accum + rounded.astype(jnp.float32)
    return accum.astype(jnp.bfloat16)


def shards(unknowns, leaf_live, near_blocks, aggregate, disaggregate, translate):
    live = leaf_live.astype(jnp.float32)[None, :, :, None, None]
    masked = (unknowns.astype(jnp.float32) * live).astype(jnp.bfloat16)
    base = complex_product("uvqn,uvnr->qr", aggregate, masked).astype(jnp.bfloat16)
    padded = with_halo(masked, (("sect", 1), ("dir", 2)), 1)
    pieces = []
    for row_step in range(-1, 2):
        for col_step in range(-1, 2):
            pieces.append(padded[:, 1 + row_step : 3 + row_step, 1 + col_step : 3 + col_step])
    beside = jnp.stack(pieces, axis=3)
    near = complex_product("uvkmn,uvknr->uvmr", near_blocks, beside)
    sect_count = lax.axis_size("sect")
    dir_count = lax.axis_size("dir")
    total_dirs = base.shape[1]
    sides = base.shape[2]
    narrow = total_dirs // (sect_count * dir_count)
    reordered = (
        base.reshape(2, dir_count, sect_count, narrow, sides)
        .transpose(0, 2, 1, 3, 4)
        .reshape(2, total_dirs, sides)[None, None]
    )
    spread = joined_exchange(reordered, ("sect", "dir"), ("sect", "dir"), (3, 3), (0, 1))
    coefs = lax.dynamic_slice_in_dim(translate, lax.axis_index("sect") * narrow, narrow, 2)
    incoming_all = translate_grid(spread, coefs)
    returned = joined_exchange(incoming_all, ("sect", "dir"), ("sect", "dir"), (0, 1), (3, 3))[0, 0]
    far = complex_product("uvmq,qr->uvmr", disaggregate, returned)
    return (near + far) * live


def solution(mesh):
    in_specs = (
        P(None, "sect", "dir", None, None),
        P("sect", "dir"),
        P(None, "sect", "dir", None, None, None),
        P(None, "sect", "dir", None, None),
        P(None, "sect", "dir", None, None),
        P(None, None, "dir"),
    )
    out_specs = P(None, "sect", "dir", None, None)
    return jax.shard_map(shards, mesh=mesh, in_specs=in_specs, out_specs=out_specs, check_vma=False)
```

profile of v0, /device:TPU:1, one launch (start us, length us, event | category | flops | bytes accessed | tf_op | source)
XLA Modules:
  0.0 100.7 jit_solution(15270804301254920206)
XLA Ops:
  0.0 1.4 %copy.104 = bf16[2,2,2,128,256]{3,4,2,1,0:T(8,128)(2,1)S(1)} copy(bf16[2,2,2,128,256]{4,3,2,1,0:T(8,128)(2,1)} %param.6) | data formatting | bytes 1048576 | tf_op args[0]
  1.4 0.7 convert_element_type.60
  2.3 5.1 %collective-permute-start.1 = (bf16[2,1,2,128,256]{3,4,2,1,0:T(8,128)(2,1)S(1)}, bf16[2,1,2,128,256]{3,4,2,1,0:T(8,128)(2,1)S(1)}, u32[]{:S(2)}, u32[]{:S(2)}) collective-permute-start(bf16[2,1,2,128,256]{3,4,2,1,0:T(8,128)(2,1)S(1)} %get-tuple-element.64), channel_id=1, source_target_pairs={{32,0},{64,32},{96,64},{128,96},{160,128},{192,160},{224,192},{33,... | collective-permute-start | bytes 786440 | tf_op jit(solution)/shard_map/ppermute | solution.py:24
  7.4 1.9 %collective-permute-start = (bf16[2,1,2,128,256]{3,4,2,1,0:T(8,128)(2,1)S(1)}, bf16[2,1,2,128,256]{3,4,2,1,0:T(8,128)(2,1)S(1)}, u32[]{:S(2)}, u32[]{:S(2)}) collective-permute-start(bf16[2,1,2,128,256]{3,4,2,1,0:T(8,128)(2,1)S(1)} %get-tuple-element.63), channel_id=1, source_target_pairs={{0,32},{32,64},{64,96},{96,128},{128,160},{160,192},{192,224},{1,3... | collective-permute-start | bytes 786440 | tf_op jit(solution)/shard_map/ppermute | solution.py:22
  9.7 1.1 %fusion.23 = bf16[512,256]{0,1:T(8,128)(2,1)} fusion(f32[256,512]{1,0:T(8,128)S(1)} %convolution_bitcast_fusion, bf16[2,2,2,512,128]{4,3,2,1,0:T(8,128)(2,1)S(1)} %copy-done, bf16[2,2,2,128,256]{3,4,2,1,0:T(8,128)(2,1)S(1)} %multiply_convert_fusion), kind=kOutput, calls=%fused_computation.33 | convolution fusion | flops 134479872 | bytes 1572864 | tf_op jit(solution)/shard_map/uvqn,uvnr->qr/dot_general | solution.py:57
  10.9 1.7 %collective-permute-done = bf16[2,1,2,128,256]{3,4,2,1,0:T(8,128)(2,1)S(1)} collective-permute-done((bf16[2,1,2,128,256]{3,4,2,1,0:T(8,128)(2,1)S(1)}, bf16[2,1,2,128,256]{3,4,2,1,0:T(8,128)(2,1)S(1)}, u32[]{:S(2)}, u32[]{:S(2)}) %collective-permute-start) | collective-permute-done | bytes 262176 | tf_op jit(solution)/shard_map/ppermute | solution.py:22
  12.8 1.1 %fusion.85 = (bf16[2,4,1,128,256]{3,4,2,1,0:T(8,128)(2,1)}, bf16[2,4,1,128,256]{3,4,2,1,0:T(8,128)(2,1)}) fusion(bf16[2,4,2,128,256]{3,4,2,1,0:T(8,128)(2,1)S(1)} %pad_maximum_fusion.1), kind=kLoop, calls=%fused_computation.182 | loop fusion | bytes 2097152 | tf_op jit(solution)/shard_map/slice | solution.py:18
  13.9 1.3 %collective-permute-start.3 = (bf16[2,4,1,128,256]{3,4,2,1,0:T(8,128)(2,1)}, bf16[2,4,1,128,256]{3,4,2,1,0:T(8,128)(2,1)}, u32[]{:S(2)}, u32[]{:S(2)}) collective-permute-start(bf16[2,4,1,128,256]{3,4,2,1,0:T(8,128)(2,1)} %get-tuple-element.59), channel_id=1, source_target_pairs={{1,0},{2,1},{3,2},{4,3},{5,4},{6,5},{7,6},{8,7},{9,8},{10,9},{11,1... | collective-permute-start | bytes 1572872 | tf_op jit(solution)/shard_map/ppermute | solution.py:24
  15.1 4.8 %collective-permute-start.2 = (bf16[2,4,1,128,256]{3,4,2,1,0:T(8,128)(2,1)}, bf16[2,4,1,128,256]{3,4,2,1,0:T(8,128)(2,1)}, u32[]{:S(2)}, u32[]{:S(2)}) collective-permute-start(bf16[2,4,1,128,256]{3,4,2,1,0:T(8,128)(2,1)} %get-tuple-element.60), channel_id=1, source_target_pairs={{0,1},{1,2},{2,3},{3,4},{4,5},{5,6},{6,7},{7,8},{8,9},{9,10},{10,1... | collective-permute-start | bytes 1572872 | tf_op jit(solution)/shard_map/ppermute | solution.py:22
  20.3 1.1 %copy.114 = bf16[512,256]{1,0:T(8,128)(2,1)S(1)} copy(bf16[512,256]{0,1:T(8,128)(2,1)} %fusion.23) | data formatting | bytes 524288 | tf_op jit(solution)/shard_map/add | solution.py:57
  21.4 0.8 stack.151
  22.2 1.0 %fusion.22 = bf16[512,256]{0,1:T(8,128)(2,1)} fusion(f32[256,512]{1,0:T(8,128)S(1)} %convolution_bitcast_fusion.2, bf16[2,2,2,512,128]{4,3,2,1,0:T(8,128)(2,1)S(1)} %copy-done, bf16[2,2,2,128,256]{3,4,2,1,0:T(8,128)(2,1)S(1)} %multiply_convert_fusion), kind=kOutput, calls=%fused_computation.32 | convolution fusion | flops 134479872 | bytes 1572864 | tf_op jit(solution)/shard_map/uvqn,uvnr->qr/dot_general | solution.py:54
  23.2 1.1 %copy.113 = bf16[512,256]{1,0:T(8,128)(2,1)S(1)} copy(bf16[512,256]{0,1:T(8,128)(2,1)} %fusion.22) | data formatting | bytes 524288 | tf_op jit(solution)/shard_map/sub | solution.py:54
  24.4 0.7 maximum_bitcast_fusion
  25.4 1.3 %copy.117 = bf16[256,1,1,2,2,256]{5,4,3,2,1,0:T(2,128)(2,1)} copy(bf16[256,1,1,2,2,256]{5,0,4,3,2,1:T(8,128)(2,1)S(1)} %bitcast.289) | data formatting | bytes 1048576 | tf_op jit(solution)/shard_map/reshape | solution.py:47
  26.7 16.5 %all-to-all-start = ((bf16[256,1,1,2,2,256]{5,4,3,2,1,0:T(2,128)(2,1)}), bf16[256,1,1,2,2,256]{5,4,3,2,1,0:T(2,128)(2,1)S(1)}, u32[]{:S(2)}, u32[]{:S(2)}) async-start(bf16[256,1,1,2,2,256]{5,4,3,2,1,0:T(2,128)(2,1)} %copy.117), calls=%async_computation | async-start | bytes 1048576 | tf_op jit(solution)/shard_map/all_to_all | solution.py:48
  43.4 1.5 %pad_maximum_fusion = (bf16[2,4,3,128,256]{3,4,2,1,0:T(8,128)(2,1)S(1)}, bf16[2,4,3,128,256]{3,4,2,1,0:T(8,128)(2,1)S(1)}) fusion(bf16[2,4,1,128,256]{3,4,2,1,0:T(8,128)(2,1)} %collective-permute-done.3, bf16[2,1,2,128,256]{3,4,2,1,0:T(8,128)(2,1)S(1)} %collective-permute-done.1, bf16[2,2,2,128,256]{3,4,2,1,0:T(8,128)(2,1)S(1)} %multiply_convert_fusion, ...), kind=kLoop, calls=%fused_computation.7 | loop fusion | flops 4718592 | bytes 5242880 | tf_op jit(solution)/shard_map/concatenate | solution.py:20
  45.8 2.1 %copy-done.3 = bf16[2,2,2,9,128,256]{4,5,3,2,1,0:T(8,128)(2,1)} copy-done((bf16[2,2,2,9,128,256]{4,5,3,2,1,0:T(8,128)(2,1)}, bf16[2,2,2,9,128,256]{4,5,3,2,1,0:T(8,128)(2,1)S(1)}, u32[]{:S(2)}) %copy-start.3) | copy-done | bytes 4718616
  48.1 0.8 fusion.7
  48.8 14.4 %all-to-all-done = bf16[256,1,1,2,2,256]{5,4,3,2,1,0:T(2,128)(2,1)S(1)} async-done(((bf16[256,1,1,2,2,256]{5,4,3,2,1,0:T(2,128)(2,1)}), bf16[256,1,1,2,2,256]{5,4,3,2,1,0:T(2,128)(2,1)S(1)}, u32[]{:S(2)}, u32[]{:S(2)}) %all-to-all-start) | async-done | bytes 524320 | tf_op jit(solution)/shard_map/all_to_all | solution.py:48
  64.1 0.6 multiply_subtract_fusion.12
  65.3 0.6 fusion.35
  65.9 0.6 multiply_subtract_fusion.15
  66.5 0.6 multiply_subtract_fusion.14
  67.1 0.9 fusion.28
  69.3 1.3 %copy.121 = bf16[256,1,1,2,2,256]{5,4,3,2,1,0:T(2,128)(2,1)} copy(bf16[256,1,1,2,2,256]{5,0,4,3,2,1:T(8,128)(2,1)S(1)} %bitcast.290) | data formatting | bytes 1048576 | tf_op jit(solution)/shard_map/reshape;transpose;transpose;reshape;reshape | solution.py:47
  70.7 6.4 %all-to-all-start.1 = ((bf16[256,1,1,2,2,256]{5,4,3,2,1,0:T(2,128)(2,1)}), bf16[256,1,1,2,2,256]{5,4,3,2,1,0:T(2,128)(2,1)S(1)}, u32[]{:S(2)}, u32[]{:S(2)}) async-start(bf16[256,1,1,2,2,256]{5,4,3,2,1,0:T(2,128)(2,1)} %copy.121), calls=%async_computation.1 | async-start | bytes 1048576 | tf_op jit(solution)/shard_map/all_to_all | solution.py:48
  77.1 2.9 %fusion.4 = f32[2,2,256,128]{3,2,1,0:T(8,128)S(1)} fusion(bf16[2,2,2,9,128,256]{4,5,3,2,1,0:T(8,128)(2,1)} %copy-done.3, bf16[2,2,2,9,128,128]{5,4,3,2,1,0:T(8,128)(2,1)} %param.8), kind=kOutput, calls=%fused_computation.8 | convolution fusion | flops 301989888 | bytes 4063232 | tf_op jit(solution)/shard_map/uvkmn,uvknr->uvmr/dot_general | solution.py:54
  80.0 2.5 %fusion.13 = f32[1,2,2,128,256]{3,4,2,1,0:T(8,128)S(1)} fusion(f32[2,2,256,128]{3,2,1,0:T(8,128)S(1)} %fusion.7, bf16[2,2,2,9,128,256]{4,5,3,2,1,0:T(8,128)(2,1)} %copy-done.3, bf16[2,2,2,9,128,128]{5,4,3,2,1,0:T(8,128)(2,1)S(1)} %copy-done.6), kind=kOutput, calls=%fused_computation.23 | convolution fusion | flops 302120960 | bytes 4587520 | tf_op jit(solution)/shard_map/uvkmn,uvknr->uvmr/dot_general | solution.py:57
  82.4 2.5 %fusion.11 = f32[1,2,2,128,256]{3,4,2,1,0:T(8,128)S(1)} fusion(f32[2,2,256,128]{3,2,1,0:T(8,128)S(1)} %fusion.4, bf16[2,2,2,9,128,256]{4,5,3,2,1,0:T(8,128)(2,1)} %copy-done.3, bf16[2,2,2,9,128,128]{5,4,3,2,1,0:T(8,128)(2,1)S(1)} %copy-done.6), kind=kOutput, calls=%fused_computation.21 | convolution fusion | flops 302120960 | bytes 4587520 | tf_op jit(solution)/shard_map/uvkmn,uvknr->uvmr/dot_general | solution.py:54
  84.9 12.3 %all-to-all-done.1 = bf16[256,1,1,2,2,256]{5,4,3,2,1,0:T(2,128)(2,1)S(1)} async-done(((bf16[256,1,1,2,2,256]{5,4,3,2,1,0:T(2,128)(2,1)}), bf16[256,1,1,2,2,256]{5,4,3,2,1,0:T(2,128)(2,1)S(1)}, u32[]{:S(2)}, u32[]{:S(2)}) %all-to-all-start.1) | async-done | bytes 524320 | tf_op jit(solution)/shard_map/all_to_all | solution.py:48
  99.4 1.3 %copy.130 = f32[2,2,2,128,256]{4,3,2,1,0:T(8,128)} copy(f32[2,2,2,128,256]{3,4,2,1,0:T(8,128)S(1)} %fusion.24) | data formatting | bytes 2097152 | tf_op jit(solution)/shard_map/mul | solution.py:111
  (51 shorter events, 7.2 us)
Async XLA Ops:
  0.0 9.4 %copy-start = (bf16[2,2,2,512,128]{4,3,2,1,0:T(8,128)(2,1)S(1)}, bf16[2,2,2,512,128]{4,3,2,1,0:T(8,128)(2,1)}, u32[]{:S(2)}) copy-start(bf16[2,2,2,512,128]{4,3,2,1,0:T(8,128)(2,1)} %param.9) | copy-start | bytes 3145732
  2.3 8.6 %collective-permute-start.1 = (bf16[2,1,2,128,256]{3,4,2,1,0:T(8,128)(2,1)S(1)}, bf16[2,1,2,128,256]{3,4,2,1,0:T(8,128)(2,1)S(1)}, u32[]{:S(2)}, u32[]{:S(2)}) collective-permute-start(bf16[2,1,2,128,256]{3,4,2,1,0:T(8,128)(2,1)S(1)} %get-tuple-element.64), channel_id=1, source_target_pairs={{32,0},{64,32},{96,64},{128,96},{160,128},{192,160},{224,192},{33,... | collective-permute-start | bytes 786440 | tf_op jit(solution)/shard_map/ppermute | solution.py:24
  7.4 5.2 %collective-permute-start = (bf16[2,1,2,128,256]{3,4,2,1,0:T(8,128)(2,1)S(1)}, bf16[2,1,2,128,256]{3,4,2,1,0:T(8,128)(2,1)S(1)}, u32[]{:S(2)}, u32[]{:S(2)}) collective-permute-start(bf16[2,1,2,128,256]{3,4,2,1,0:T(8,128)(2,1)S(1)} %get-tuple-element.63), channel_id=1, source_target_pairs={{0,32},{32,64},{64,96},{96,128},{128,160},{160,192},{192,224},{1,3... | collective-permute-start | bytes 786440 | tf_op jit(solution)/shard_map/ppermute | solution.py:22
  13.9 29.6 %collective-permute-start.3 = (bf16[2,4,1,128,256]{3,4,2,1,0:T(8,128)(2,1)}, bf16[2,4,1,128,256]{3,4,2,1,0:T(8,128)(2,1)}, u32[]{:S(2)}, u32[]{:S(2)}) collective-permute-start(bf16[2,4,1,128,256]{3,4,2,1,0:T(8,128)(2,1)} %get-tuple-element.59), channel_id=1, source_target_pairs={{1,0},{2,1},{3,2},{4,3},{5,4},{6,5},{7,6},{8,7},{9,8},{10,9},{11,1... | collective-permute-start | bytes 1572872 | tf_op jit(solution)/shard_map/ppermute | solution.py:24
  15.1 28.3 %collective-permute-start.2 = (bf16[2,4,1,128,256]{3,4,2,1,0:T(8,128)(2,1)}, bf16[2,4,1,128,256]{3,4,2,1,0:T(8,128)(2,1)}, u32[]{:S(2)}, u32[]{:S(2)}) collective-permute-start(bf16[2,4,1,128,256]{3,4,2,1,0:T(8,128)(2,1)} %get-tuple-element.60), channel_id=1, source_target_pairs={{0,1},{1,2},{2,3},{3,4},{4,5},{5,6},{6,7},{7,8},{8,9},{9,10},{10,1... | collective-permute-start | bytes 1572872 | tf_op jit(solution)/shard_map/ppermute | solution.py:22
  22.2 2.2 %copy-start.2 = (bf16[1,32,8,2,256]{4,3,2,1,0:T(2,128)(2,1)S(1)}, bf16[1,32,8,2,256]{4,3,2,1,0:T(2,128)(2,1)}, u32[]{:S(2)}) copy-start(bf16[1,32,8,2,256]{4,3,2,1,0:T(2,128)(2,1)} %stack.151) | copy-start | bytes 786436
  24.3 18.9 %copy-start.4 = (f32[16,2,16]{2,1,0:T(2,128)S(1)}, f32[16,2,16]{2,1,0:T(2,128)}, u32[]{:S(2)}) copy-start(f32[16,2,16]{2,1,0:T(2,128)} %param.11) | copy-start | bytes 6148
  26.7 36.6 %all-to-all-start = ((bf16[256,1,1,2,2,256]{5,4,3,2,1,0:T(2,128)(2,1)}), bf16[256,1,1,2,2,256]{5,4,3,2,1,0:T(2,128)(2,1)S(1)}, u32[]{:S(2)}, u32[]{:S(2)}) async-start(bf16[256,1,1,2,2,256]{5,4,3,2,1,0:T(2,128)(2,1)} %copy.117), calls=%async_computation | async-start | bytes 1048576 | tf_op jit(solution)/shard_map/all_to_all | solution.py:48
  45.5 2.6 %copy-start.5 = (bf16[2,2,2,9,128,128]{5,4,3,2,1,0:T(8,128)(2,1)S(1)}, bf16[2,2,2,9,128,128]{5,4,3,2,1,0:T(8,128)(2,1)}, u32[]{:S(2)}) copy-start(bf16[2,2,2,9,128,128]{5,4,3,2,1,0:T(8,128)(2,1)} %param.8) | copy-start | bytes 7077892
  45.8 2.1 %copy-start.3 = (bf16[2,2,2,9,128,256]{4,5,3,2,1,0:T(8,128)(2,1)}, bf16[2,2,2,9,128,256]{4,5,3,2,1,0:T(8,128)(2,1)S(1)}, u32[]{:S(2)}) copy-start(bf16[2,2,2,9,128,256]{4,5,3,2,1,0:T(8,128)(2,1)S(1)} %fusion.40) | copy-start | bytes 14155780
  70.7 26.6 %all-to-all-start.1 = ((bf16[256,1,1,2,2,256]{5,4,3,2,1,0:T(2,128)(2,1)}), bf16[256,1,1,2,2,256]{5,4,3,2,1,0:T(2,128)(2,1)S(1)}, u32[]{:S(2)}, u32[]{:S(2)}) async-start(bf16[256,1,1,2,2,256]{5,4,3,2,1,0:T(2,128)(2,1)} %copy.121), calls=%async_computation.1 | async-start | bytes 1048576 | tf_op jit(solution)/shard_map/all_to_all | solution.py:48
  77.1 2.9 %copy-start.6 = (bf16[2,2,2,9,128,128]{5,4,3,2,1,0:T(8,128)(2,1)S(1)}, bf16[2,2,2,9,128,128]{5,4,3,2,1,0:T(8,128)(2,1)}, u32[]{:S(2)}) copy-start(bf16[2,2,2,9,128,128]{5,4,3,2,1,0:T(8,128)(2,1)} %param.8) | copy-start | bytes 7077892
  84.9 12.8 %copy-start.1 = (bf16[2,2,2,128,512]{4,3,2,1,0:T(8,128)(2,1)S(1)}, bf16[2,2,2,128,512]{4,3,2,1,0:T(8,128)(2,1)}, u32[]{:S(2)}) copy-start(bf16[2,2,2,128,512]{4,3,2,1,0:T(8,128)(2,1)} %param.10) | copy-start | bytes 3145732
where the time goes:
time: 101 us
  starting transfers between devices  36 us (36%)
  waiting for transfers between devices  28.6 us (28%)
  local copies, waits for them, and re-layouts  13.1 us (13%)
  matrix products  12.7 us (13%)
  other arithmetic  9.68 us (10%)
    all_to_all x2, waiting for transfers between devices, joined_exchange(): tiles = lax.all_to_all(tiles, axis, split_axis=0, concat_axis=0, tiled=True)  26.8 us
    all_to_all x2, starting transfers between devices, joined_exchange(): tiles = lax.all_to_all(tiles, axis, split_axis=0, concat_axis=0, tiled=True)  22.9 us
    ppermute x2, starting transfers between devices, with_halo(): lax.ppermute(tail, axis, [(i, (i + 1) % count) for i in range(ends)])  6.72 us
    ppermute x2, starting transfers between devices, with_halo(): lax.ppermute(head, axis, [((i + 1) % count, i) for i in range(ends)])  6.39 us
    unnamed x20, local copies, waits for them, and re-layouts  4.01 us
    dot_general x3, matrix products, complex_product(): jnp.einsum(form, left[0], right[1], preferred_element_type=jnp.float32)  3.86 us
    dot_general x3, matrix products, complex_product(): jnp.einsum(form, left[0], right[0], preferred_element_type=jnp.float32)  3.83 us
    dot_general x3, matrix products, complex_product(): jnp.einsum(form, left[1], right[1], preferred_element_type=jnp.float32)  3.58 us
  transfers between devices with their start and end apart: 6, of which 4 were waited for; matrix products, arithmetic and copies ran while one was open for 19% of the time, Pallas kernels for 0%

commit v1 on v0

v1 whole, which is shorter than its diff:
```python
import functools

import jax
import jax.numpy as jnp
from jax import lax
from jax.experimental import pallas as pl
from jax.experimental.pallas import tpu as pltpu
from jax.sharding import PartitionSpec as P

MESH = pl.DeviceIdType.MESH
PLANE_COLS = 4
LANES = 128

far_offsets = [(a, b) for a in range(-2, 3) for b in range(-2, 3) if max(abs(a), abs(b)) == 2]


def stacked(real, imag, axis=0):
    top = jnp.concatenate([real, imag], axis=1)
    low = jnp.concatenate([-imag, real], axis=1)
    return jnp.concatenate([top, low], axis=0)


def dot(left, right):
    return jnp.dot(left, right, preferred_element_type=jnp.float32)


def kernel(
    ns, nd, live_ref, unk_hbm, nb_hbm, agg_hbm, dis_hbm, tr_ref, out_hbm,
    raw, leaves, nb, agg, dis, pat, grid, inc, back, acc, trs, trd, coef,
    load_sem, nx_sem, ny_sem, t_sem, s1_sem, r1_sem, sz_sem, rz_sem, s2_sem, r2_sem, out_sem,
):
    nx = PLANE_COLS
    nz = nd // nx
    owners = ns * nx
    total_dirs = agg.shape[3]
    nq = total_dirs // owners
    f32, bf16 = jnp.float32, jnp.bfloat16

    s, d = lax.axis_index("sect"), lax.axis_index("dir")
    z, x = d // nx, lax.rem(d, nx)
    me = s * nx + x

    loads = [
        pltpu.make_async_copy(src, dst, load_sem.at[i])
        for i, (src, dst) in enumerate(((unk_hbm, raw), (agg_hbm, agg), (nb_hbm, nb), (dis_hbm, dis)))
    ]
    loads[0].start()
    loads[1].start()

    def owner_device(t):
        return (t // nx, z * nx + lax.rem(t, nx))

    bar = pltpu.get_barrier_semaphore()

    def greet(device):
        pl.semaphore_signal(bar, inc=1, device_id=device, device_id_type=MESH)

    @pl.loop(1, owners)
    def _(i):
        greet(owner_device(lax.rem(me + i, owners)))

    for step in (1, nz - 1):
        greet((s, lax.rem(z + step, nz) * nx + x))
    for step in (1, nd - 1):
        greet((s, lax.rem(d + step, nd)))

    @pl.when(s != z)
    def _():
        greet((z, s * nx + x))

    def clear(ref):
        ref[...] = jnp.zeros(ref.shape, ref.dtype)

    @pl.when(s == 0)
    def _():
        clear(leaves.at[0])

    @pl.when(s == ns - 1)
    def _():
        clear(leaves.at[3])

    @pl.when(d == 0)
    def _():
        clear(leaves.at[1:3, 0])

    @pl.when(d == nd - 1)
    def _():
        clear(leaves.at[1:3, 3])

    for rc in range(2):
        clear(grid.at[rc, 0:2])
        clear(grid.at[rc, ns + 2 : ns + 4])

    @pl.when(z == 0)
    def _():
        for rc in range(2):
            clear(grid.at[rc, 2 : ns + 2, 0:2])

    @pl.when(z == nz - 1)
    def _():
        for rc in range(2):
            clear(grid.at[rc, 2 : ns + 2, nx + 2 : nx + 4])

    clear(trs)
    for k in range(16):
        trs[2 * k : 2 * k + 2, 0:nq] = tr_ref[k]
    loads[0].wait()
    loads[2].start()
    loads[3].start()
    for i in range(2):
        for j in range(2):
            live = live_ref[i, j].astype(f32)
            for c in range(2):
                leaves[1 + i, 1 + j, c] = (raw[c, i, j].astype(f32) * live).astype(bf16)

    pl.semaphore_wait(bar, owners - 1 + 4 + jnp.where(s != z, 1, 0))

    def remote(src, dst, sems, i, device):
        return pltpu.make_async_remote_copy(
            src_ref=src, dst_ref=dst, send_sem=sems.at[0, i], recv_sem=sems.at[1, i],
            device_id=device, device_id_type=MESH,
        )

    swap = remote(trs, trd, t_sem, 0, (z, s * nx + x))

    @pl.when(s != z)
    def _():
        swap.start()

    @pl.when(s == z)
    def _():
        trd[...] = trs[...]

    to_left = remote(leaves.at[1:3, 1], leaves.at[1:3, 3], nx_sem, 0, (s, d - 1))
    to_right = remote(leaves.at[1:3, 2], leaves.at[1:3, 0], nx_sem, 1, (s, d + 1))

    spans = ((1, 3), (0, 1), (3, 4))
    up = [
        remote(leaves.at[1, a:b], leaves.at[3, a:b], ny_sem, i, (s - 1, d)) for i, (a, b) in enumerate(spans)
    ]
    down = [
        remote(leaves.at[2, a:b], leaves.at[0, a:b], ny_sem, 3 + i, (s + 1, d)) for i, (a, b) in enumerate(spans)
    ]

    def start_columns():
        @pl.when(d > 0)
        def _():
            to_left.start()

        @pl.when(d < nd - 1)
        def _():
            to_right.start()

    def start_rows(which):
        @pl.when(s > 0)
        def _():
            for i in which:
                up[i].start()

        @pl.when(s < ns - 1)
        def _():
            for i in which:
                down[i].start()

    def lanes(rc):
        return pl.ds(rc * LANES, LANES)

    def dirs_of(t):
        return pl.ds(pl.multiple_of(t * nq, nq), nq)

    loads[1].wait()
    for rc in range(2):
        cols = slice(rc * LANES, (rc + 1) * LANES)
        right = stacked(
            *[
                jnp.concatenate([leaves[1 + i, 1 + j, c, :, cols] for i in range(2) for j in range(2)], axis=0)
                for c in range(2)
            ]
        )
        rows = min(256, total_dirs)
        for q0 in range(0, total_dirs, rows):
            left = jnp.concatenate(
                [agg[c, i, j, q0 : q0 + rows] for c in range(2) for i in range(2) for j in range(2)], axis=1
            )
            both = dot(left, right)
            for c in range(2):
                pat[c, q0 : q0 + rows, cols] = both[:, c * LANES : (c + 1) * LANES].astype(bf16)

        @pl.loop(1, owners)
        def _(i, rc=rc):
            t = lax.rem(me + i, owners)
            pltpu.make_async_remote_copy(
                src_ref=pat.at[:, dirs_of(t), lanes(rc)],
                dst_ref=grid.at[rc, 2 + s, 2 + x],
                send_sem=s1_sem.at[rc],
                recv_sem=r1_sem.at[rc, x // 2],
                device_id=owner_device(t),
                device_id_type=MESH,
            ).start()

        pltpu.make_async_copy(
            pat.at[:, dirs_of(me), lanes(rc)], grid.at[rc, 2 + s, 2 + x], r1_sem.at[rc, x // 2]
        ).start()
        if rc == 0:
            start_columns()

    start_rows((0,))

    def near(p, q, first=False):
        right = stacked(leaves[p, q, 0], leaves[p, q, 1])
        targets = [(i, j) for i in range(2) for j in range(2) if 0 <= p - i <= 2 and 0 <= q - j <= 2]
        left = jnp.concatenate(
            [
                jnp.concatenate([nb[c, i, j, 3 * (p - i) + q - j] for c in range(2)], axis=1)
                for i, j in targets
            ],
            axis=0,
        )
        both = dot(left, right)
        rows = left.shape[0] // len(targets)
        width = both.shape[1] // 2
        for n, (i, j) in enumerate(targets):
            for c in range(2):
                part = both[n * rows : (n + 1) * rows, c * width : (c + 1) * width]
                acc[c, i, j] = part if first else acc[c, i, j] + part

    loads[2].wait()
    for n, (p, q) in enumerate(((1, 1), (1, 2), (2, 1), (2, 2))):
        near(p, q, n == 0)

    @pl.when(d < nd - 1)
    def _():
        to_left.wait_recv()

    @pl.when(d > 0)
    def _():
        to_right.wait_recv()

    start_rows((1, 2))

    def plane(rc, side):
        own = grid.at[rc, 2 : ns + 2, 2:4] if side == 0 else grid.at[rc, 2 : ns + 2, nx : nx + 2]
        there = grid.at[rc, 2 : ns + 2, nx + 2 : nx + 4] if side == 0 else grid.at[rc, 2 : ns + 2, 0:2]
        return pltpu.make_async_remote_copy(
            src_ref=own, dst_ref=there, send_sem=sz_sem.at[rc, side], recv_sem=rz_sem.at[rc, side],
            device_id=(s, d - nx if side == 0 else d + nx), device_id_type=MESH,
        )

    for rc in range(2):
        for side in range(2):
            half = grid.at[rc, 2 : ns + 2, 2 + 2 * side : 4 + 2 * side]
            pltpu.make_async_copy(half, half, r1_sem.at[rc, side]).wait()

            @pl.when(z > 0 if side == 0 else z < nz - 1)
            def _(rc=rc, side=side):
                plane(rc, side).start()

        if rc == 0:
            @pl.when(s != z)
            def _():
                swap.wait_recv()

            turned = trd[...].T
            for k in range(32):
                coef[k] = jnp.broadcast_to(turned[0:nq, k : k + 1], (nq, LANES))

    for rc in range(2):

        @pl.when(z < nz - 1)
        def _(rc=rc):
            plane(rc, 0).wait_recv()

        @pl.when(z > 0)
        def _(rc=rc):
            plane(rc, 1).wait_recv()

        @pl.loop(0, ns)
        def _(target, rc=rc):
            total = [jnp.zeros((nx, nq, LANES), f32) for _ in range(2)]
            for row_step in range(-2, 3):
                term = [jnp.zeros((nx, nq, LANES), f32) for _ in range(2)]
                for k, (a, b) in enumerate(far_offsets):
                    if a == row_step:
                        u, v = (
                            grid[rc, target + 2 + a, 2 + b : 2 + b + nx, c].astype(f32) for c in range(2)
                        )
                        p, q = coef[2 * k][None], coef[2 * k + 1][None]
                        term[0] += p * u - q * v
                        term[1] += p * v + q * u
                for c in range(2):
                    total[c] += term[c].astype(bf16).astype(f32)
            for col in range(nx):
                for c in range(2):
                    inc[rc, target * nx + col, c] = total[c][col].astype(bf16)

        @pl.loop(1, owners)
        def _(i, rc=rc):
            t = lax.rem(me + i, owners)
            pltpu.make_async_remote_copy(
                src_ref=inc.at[rc, t],
                dst_ref=back.at[:, dirs_of(me), lanes(rc)],
                send_sem=s2_sem.at[rc],
                recv_sem=r2_sem.at[rc],
                device_id=owner_device(t),
                device_id_type=MESH,
            ).start()

        pltpu.make_async_copy(inc.at[rc, me], back.at[:, dirs_of(me), lanes(rc)], r2_sem.at[rc]).start()

    @pl.when(s < ns - 1)
    def _():
        for copy in up:
            copy.wait_recv()

    @pl.when(s > 0)
    def _():
        for copy in down:
            copy.wait_recv()

    for p in range(4):
        for q in range(4):
            if p in (0, 3) or q in (0, 3):
                near(p, q)

    loads[3].wait()
    outs = []
    for rc in range(2):
        cols = slice(rc * LANES, (rc + 1) * LANES)
        whole = back.at[:, :, cols]
        pltpu.make_async_copy(whole, whole, r2_sem.at[rc]).wait()
        right = stacked(back[0, :, cols], back[1, :, cols])
        for i in range(2):
            left = jnp.concatenate(
                [jnp.concatenate([dis[c, i, j] for c in range(2)], axis=1) for j in range(2)], axis=0
            )
            both = dot(left, right)
            rows = left.shape[0] // 2
            for j in range(2):
                live = live_ref[i, j].astype(f32)
                for c in range(2):
                    part = both[j * rows : (j + 1) * rows, c * LANES : (c + 1) * LANES]
                    acc[c, i, j, :, cols] = (acc[c, i, j, :, cols] + part) * live
        copy = pltpu.make_async_copy(acc.at[..., cols], out_hbm.at[..., cols], out_sem.at[rc])
        copy.start()
        outs.append(copy)

    @pl.when(s != z)
    def _():
        swap.wait_send()

    @pl.when(d > 0)
    def _():
        to_left.wait_send()

    @pl.when(d < nd - 1)
    def _():
        to_right.wait_send()

    @pl.when(s > 0)
    def _():
        for copy in up:
            copy.wait_send()

    @pl.when(s < ns - 1)
    def _():
        for copy in down:
            copy.wait_send()

    for rc in range(2):
        sent = inc.at[rc, 0 : owners - 1]
        pltpu.make_async_copy(sent, sent, s1_sem.at[rc]).wait()
        pltpu.make_async_copy(sent, sent, s2_sem.at[rc]).wait()

        @pl.when(z > 0)
        def _(rc=rc):
            plane(rc, 0).wait_send()

        @pl.when(z < nz - 1)
        def _(rc=rc):
            plane(rc, 1).wait_send()

        outs[rc].wait()


def shards(ns, nd, unknowns, leaf_live, near_blocks, aggregate, disaggregate, translate):
    nq = translate.shape[2]
    leaf, sides = unknowns.shape[3:]
    dirs = aggregate.shape[3]
    bf16, f32 = jnp.bfloat16, jnp.float32
    owners = ns * PLANE_COLS
    any_space = pl.BlockSpec(memory_space=pl.ANY)
    dma = pltpu.SemaphoreType.DMA
    field = pl.pallas_call(
        functools.partial(kernel, ns, nd),
        out_shape=jax.ShapeDtypeStruct(unknowns.shape, f32),
        in_specs=[
            pl.BlockSpec(memory_space=pltpu.SMEM),
            any_space,
            any_space,
            any_space,
            any_space,
            pl.BlockSpec(memory_space=pltpu.VMEM),
        ],
        out_specs=any_space,
        scratch_shapes=[
            pltpu.VMEM(unknowns.shape, bf16),
            pltpu.VMEM((4, 4, 2, leaf, sides), bf16),
            pltpu.VMEM(near_blocks.shape, bf16),
            pltpu.VMEM(aggregate.shape, bf16),
            pltpu.VMEM(disaggregate.shape, bf16),
            pltpu.VMEM((2, dirs, sides), bf16),
            pltpu.VMEM((2, ns + 4, PLANE_COLS + 4, 2, nq, LANES), bf16),
            pltpu.VMEM((2, owners, 2, nq, LANES), bf16),
            pltpu.VMEM((2, dirs, sides), bf16),
            pltpu.VMEM(unknowns.shape, f32),
            pltpu.VMEM((32, LANES), f32),
            pltpu.VMEM((32, LANES), f32),
            pltpu.VMEM((32, nq, LANES), f32),
            dma((4,)),
            dma((2, 2)),
            dma((2, 6)),
            dma((2, 1)),
            dma((2,)),
            dma((2, 2)),
            dma((2, 2)),
            dma((2, 2)),
            dma((2,)),
            dma((2,)),
            dma((2,)),
        ],
        compiler_params=pltpu.CompilerParams(
            collective_id=0, has_side_effects=True, vmem_limit_bytes=56 * 1024 * 1024
        ),
    )(leaf_live, unknowns, near_blocks, aggregate, disaggregate, translate)
    return field


def solution(mesh):
    in_specs = (
        P(None, "sect", "dir", None, None),
        P("sect", "dir"),
        P(None, "sect", "dir", None, None, None),
        P(None, "sect", "dir", None, None),
        P(None, "sect", "dir", None, None),
        P(None, None, "dir"),
    )
    out_specs = P(None, "sect", "dir", None, None)
    body = functools.partial(shards, mesh.shape["sect"], mesh.shape["dir"])
    return jax.shard_map(body, mesh=mesh, in_specs=in_specs, out_specs=out_specs, check_vma=False)
```

time: 101 us -> 41.8 us (0.41)
  Pallas kernels: 0 us -> 39.4 us
  starting transfers between devices: 36 us -> 0 us
  waiting for transfers between devices: 28.6 us -> 0 us
  matrix products: 12.7 us -> 0 us
  local copies, waits for them, and re-layouts: 13.1 us -> 2.27 us
  other arithmetic: 9.68 us -> 0 us
    pallas_call x0 -> x1, Pallas kernels: none -> 39.4 us  [shards(): pl.pallas_call(functools.partial(kernel, ns, nd), out_shape=jax.ShapeDtyp...]
    all_to_all x2 -> x0, waiting for transfers between devices: 26.8 us -> none  [joined_exchange(): tiles = lax.all_to_all(tiles, axis, split_axis=0, concat_axis=0, tiled=True)]
    all_to_all x2 -> x0, starting transfers between devices: 22.9 us -> none  [joined_exchange(): tiles = lax.all_to_all(tiles, axis, split_axis=0, concat_axis=0, tiled=True)]
    ppermute x4 -> x0, starting transfers between devices: 13.1 us -> none  [the longest x2 6.72 us: with_halo(): lax.ppermute(tail, axis, [(i, (i + 1) % count) for i in range(ends)])]
    dot_general x12 -> x0, matrix products: 12.7 us -> none  [the longest x3 3.86 us: complex_product(): jnp.einsum(form, left[0], right[1], preferred_element_type=jnp.float32)]
    convert_element_type x6 -> x0, other arithmetic: 3.46 us -> none  [the longest x3 2.12 us: translate_grid(): rounded = lax.optimization_barrier(total.astype(jnp.bfloat16))]
    sub x6 -> x0, other arithmetic: 3.02 us -> none  [translate_grid(): real = coef_real * shifted[:, :, 0] - coef_imag * shifted[:, :, 1]]
    another operation x5 -> x0, local copies, waits for them, and re-layouts: 2.49 us -> none  [the longest x1 1.33 us: joined_exchange(): tiles = tiles.reshape(-1, *inside)]
  transfers between devices with their start and end apart: 6 -> 0, of which waited for: 4 -> 0; matrix products, arithmetic and copies ran while one was open for 19% -> 0% of each run, Pallas kernels for 0% -> 0%
where the time goes in v1:
time: 41.8 us; the launch traced here: 41.6 us
  Pallas kernels  39.4 us (94%)
  local copies, waits for them, and re-layouts  2.27 us (5%)
    pallas_call x1, Pallas kernels, shards(): pl.pallas_call(functools.partial(kernel, ns, nd), out_shape=jax.ShapeDtyp...  39.4 us
    unnamed x1, local copies, waits for them, and re-layouts  2.27 us

profile of v1, /device:TPU:1, one launch (start us, length us, event | category | flops | bytes accessed | tf_op | source)
XLA Modules:
  0.0 41.6 jit_solution(9799082708237989122)
XLA Ops:
  0.0 39.4 %shard_map.64 = f32[2,2,2,128,256]{4,3,2,1,0:T(8,128)} custom-call(s32[2,2]{1,0:T(2,128)} %live_ref.1, bf16[2,2,2,128,256]{4,3,2,1,0:T(8,128)(2,1)} %unk_hbm.1, bf16[2,2,2,9,128,128]{5,4,3,2,1,0:T(8,128)(2,1)} %nb_hbm.1, bf16[2,2,2,512,128]{4,3,2,1,0:T(8,128)(2,1)} %agg_hbm.1, bf16[2,2,2,128,512]{4,3,2,1,0:T(8,128)(2,1)} %dis_hbm.1, f32[16,2,16]{2,1,0:T(2,128)} %tr_ref.1), custom_call_target="tpu_custom_call" | custom-call | tf_op jit(solution)/shard_map/pallas_call | solution.py:393
  39.4 2.3 %copy.8 = f32[2,2,2,128,256]{4,3,2,1,0:T(8,128)} copy(f32[2,2,2,128,256]{4,3,2,1,0:T(8,128)} %shard_map.64) | data formatting | bytes 2097152

commit v2 on v1

v2 whole, which is shorter than its diff:
```python
import functools

import jax
import jax.numpy as jnp
from jax import lax
from jax.experimental import pallas as pl
from jax.experimental.pallas import tpu as pltpu
from jax.sharding import PartitionSpec as P

MESH = pl.DeviceIdType.MESH
PLANE_COLS = 4
LANES = 128

far_offsets = [(a, b) for a in range(-2, 3) for b in range(-2, 3) if max(abs(a), abs(b)) == 2]


def stacked(real, imag, axis=0):
    top = jnp.concatenate([real, imag], axis=1)
    low = jnp.concatenate([-imag, real], axis=1)
    return jnp.concatenate([top, low], axis=0)


def dot(left, right):
    return jnp.dot(left, right, preferred_element_type=jnp.float32)


def kernel(
    ns, nd, live_ref, unk_hbm, nb_hbm, agg_hbm, dis_hbm, tr_ref, acc,
    raw, leaves, hop, nb, agg, dis, pat, grid, inc, back, trs, trd, mix,
    load_sem, hop_sem, nx_sem, ny_sem, t_sem, s1_sem, r1_sem, sz_sem, rz_sem, s2_sem, r2_sem,
):
    nx = PLANE_COLS
    nz = nd // nx
    owners = ns * nx
    total_dirs = agg.shape[3]
    nq = total_dirs // owners
    f32, bf16 = jnp.float32, jnp.bfloat16

    s, d = lax.axis_index("sect"), lax.axis_index("dir")
    z, x = d // nx, lax.rem(d, nx)
    me = s * nx + x

    loads = [
        pltpu.make_async_copy(src, dst, load_sem.at[i])
        for i, (src, dst) in enumerate(((unk_hbm, raw), (agg_hbm, agg), (nb_hbm, nb), (dis_hbm, dis)))
    ]
    loads[0].start()
    loads[1].start()

    def owner_device(t):
        return (t // nx, z * nx + lax.rem(t, nx))

    ny = ns // 2
    y, core = s // 2, lax.rem(s, 2)
    y_order = sorted(range(ny), key=lambda step: (-min(step, ny - step), step))
    x_order = sorted(range(nx), key=lambda step: (-min(step, nx - step), step))
    y_digits = sum(step * 4**i for i, step in enumerate(y_order))

    def far_row(i):
        step = lax.rem(lax.shift_right_logical(jnp.int32(y_digits), 2 * (i // 2)), 4)
        return lax.rem(y + step, ny) * 2 + lax.rem(core + 1 + lax.rem(i, 2), 2)

    def far_columns():
        return [lax.rem(x + step, nx) for step in x_order]

    bar = pltpu.get_barrier_semaphore()

    def greet(device):
        pl.semaphore_signal(bar, inc=1, device_id=device, device_id_type=MESH)

    @pl.when(s != z)
    def _():
        greet((z, s * nx + x))

    def hops(step):
        return min(step[0], ny - step[0]) + min(step[2], nx - step[2])

    steps = [(a, b, c) for a in range(ny) for b in range(2) for c in range(nx)][1:]
    for a, b, c in sorted(steps, key=lambda step: -hops(step)):
        greet((lax.rem(y + a, ny) * 2 + lax.rem(core + b, 2), z * nx + lax.rem(x + c, nx)))
    for step in (1, nz - 1):
        greet((s, lax.rem(z + step, nz) * nx + x))

    def clear(ref):
        ref[...] = jnp.zeros(ref.shape, ref.dtype)

    @pl.when(s == 0)
    def _():
        clear(leaves.at[0])

    @pl.when(s == ns - 1)
    def _():
        clear(leaves.at[3])

    @pl.when(d == 0)
    def _():
        clear(leaves.at[1:3, 0])

    @pl.when(d == nd - 1)
    def _():
        clear(leaves.at[1:3, 3])

    clear(trs)
    for k in range(16):
        trs[2 * k : 2 * k + 2, 0:nq] = tr_ref[k]
    loads[0].wait()
    loads[2].start()
    loads[3].start()
    for i in range(2):
        for j in range(2):
            live = live_ref[i, j].astype(f32)
            for c in range(2):
                leaves[1 + i, 1 + j, c] = (raw[c, i, j].astype(f32) * live).astype(bf16)

    loads[1].wait()
    for rc in range(2):
        cols = slice(rc * LANES, (rc + 1) * LANES)
        right = stacked(
            *[
                jnp.concatenate([leaves[1 + i, 1 + j, c, :, cols] for i in range(2) for j in range(2)], axis=0)
                for c in range(2)
            ]
        )
        rows = min(256, total_dirs)
        for q0 in range(0, total_dirs, rows):
            left = jnp.concatenate(
                [agg[c, i, j, q0 : q0 + rows] for c in range(2) for i in range(2) for j in range(2)], axis=1
            )
            both = dot(left, right)
            for c in range(2):
                pat[c, q0 : q0 + rows, cols] = both[:, c * LANES : (c + 1) * LANES].astype(bf16)

    pl.semaphore_wait(bar, owners - 1 + 2 + jnp.where(s != z, 1, 0))

    def remote(src, dst, sems, i, device):
        return pltpu.make_async_remote_copy(
            src_ref=src, dst_ref=dst, send_sem=sems.at[0, i], recv_sem=sems.at[1, i],
            device_id=device, device_id_type=MESH,
        )

    swap = remote(trs, trd, t_sem, 0, (z, s * nx + x))

    @pl.when(s != z)
    def _():
        swap.start()

    @pl.when(s == z)
    def _():
        trd[...] = trs[...]

    left_end, right_end = x == 0, x == nx - 1
    before, after = z > 0, z < nz - 1
    left = (s, z * nx + jnp.where(left_end, nx - 1, x - 1))
    right = (s, z * nx + jnp.where(right_end, 0, x + 1))
    prev, nxt = (s, d - nx), (s, d + nx)

    def to_left(r, src=None):
        return remote(leaves.at[1 + r, 1] if src is None else src, leaves.at[1 + r, 3], nx_sem, r, left)

    def to_right(r, src=None):
        return remote(leaves.at[1 + r, 2] if src is None else src, leaves.at[1 + r, 0], nx_sem, 2 + r, right)

    first_left = remote(leaves.at[1, 1], hop.at[0], hop_sem, 0, prev)
    first_right = remote(leaves.at[1, 2], hop.at[0], hop_sem, 0, nxt)
    second_left = remote(leaves.at[2, 1], hop.at[1], hop_sem, 1, left)
    second_right = remote(leaves.at[2, 2], hop.at[1], hop_sem, 1, right)

    def pass_on(column, recv, device):
        return pltpu.make_async_remote_copy(
            src_ref=hop.at[1], dst_ref=leaves.at[2, column], send_sem=hop_sem.at[0, 2], recv_sem=nx_sem.at[1, recv],
            device_id=device, device_id_type=MESH,
        )


    spans = ((1, 3), (0, 1), (3, 4))
    up = [
        remote(leaves.at[1, a:b], leaves.at[3, a:b], ny_sem, i, (s - 1, d)) for i, (a, b) in enumerate(spans)
    ]
    down = [
        remote(leaves.at[2, a:b], leaves.at[0, a:b], ny_sem, 3 + i, (s + 1, d)) for i, (a, b) in enumerate(spans)
    ]

    def start_columns():
        for r in range(2):

            @pl.when(jnp.logical_not(left_end))
            def _(r=r):
                to_left(r).start()

            @pl.when(jnp.logical_not(right_end))
            def _(r=r):
                to_right(r).start()

        @pl.when(left_end & before)
        def _():
            second_left.start()

        @pl.when(right_end & after)
        def _():
            second_right.start()

    def start_hops():
        @pl.when(left_end & before)
        def _():
            first_left.start()

        @pl.when(right_end & after)
        def _():
            first_right.start()

    def pass_first():
        @pl.when(left_end & after)
        def _():
            first_left.wait_recv()
            to_left(0, hop.at[0]).start()

        @pl.when(right_end & before)
        def _():
            first_right.wait_recv()
            to_right(0, hop.at[0]).start()

    def pass_second():
        @pl.when(right_end & before)
        def _():
            second_left.wait_recv()
            pass_on(3, 1, prev).start()

        @pl.when(left_end & after)
        def _():
            second_right.wait_recv()
            pass_on(0, 3, nxt).start()

    def columns_came(r):
        @pl.when(d < nd - 1)
        def _():
            to_left(r).wait_recv()

        @pl.when(d > 0)
        def _():
            to_right(r).wait_recv()

    def start_up(which):
        @pl.when(s > 0)
        def _():
            for i in which:
                up[i].start()

    def start_down(which):
        @pl.when(s < ns - 1)
        def _():
            for i in which:
                down[i].start()

    def lanes(rc):
        return pl.ds(rc * LANES, LANES)

    def dirs_of(t):
        return pl.ds(pl.multiple_of(t * nq, nq), nq)

    start_hops()

    for rc in range(2):

        @pl.loop(0, ns)
        def _(i, rc=rc):
            row = far_row(i)
            for col in far_columns():
                t = row * nx + col
                src, dst = pat.at[:, dirs_of(t), lanes(rc)], grid.at[rc, 2 + s, 2 + x]
                arrived = r1_sem.at[rc, x // 2, y]

                @pl.when(t != me)
                def _(t=t, src=src):
                    pltpu.make_async_remote_copy(
                        src_ref=src, dst_ref=dst, send_sem=s1_sem.at[rc], recv_sem=arrived,
                        device_id=owner_device(t), device_id_type=MESH,
                    ).start()

                @pl.when(t == me)
                def _(src=src):
                    pltpu.make_async_copy(src, dst, arrived).start()

    start_columns()
    start_up((0,))
    start_down((0,))
    for rc in range(2):
        clear(grid.at[rc, 0:2])
        clear(grid.at[rc, ns + 2 : ns + 4])

    @pl.when(z == 0)
    def _():
        for rc in range(2):
            clear(grid.at[rc, 2 : ns + 2, 0:2])

    @pl.when(z == nz - 1)
    def _():
        for rc in range(2):
            clear(grid.at[rc, 2 : ns + 2, nx + 2 : nx + 4])

    def near(p, q, first=False):
        right = stacked(leaves[p, q, 0], leaves[p, q, 1])
        targets = [(i, j) for i in range(2) for j in range(2) if 0 <= p - i <= 2 and 0 <= q - j <= 2]
        left = jnp.concatenate(
            [
                jnp.concatenate([nb[c, i, j, 3 * (p - i) + q - j] for c in range(2)], axis=1)
                for i, j in targets
            ],
            axis=0,
        )
        both = dot(left, right)
        rows = left.shape[0] // len(targets)
        width = both.shape[1] // 2
        for n, (i, j) in enumerate(targets):
            for c in range(2):
                part = both[n * rows : (n + 1) * rows, c * width : (c + 1) * width]
                acc[c, i, j] = part if first else acc[c, i, j] + part

    loads[2].wait()
    for n, (p, q) in enumerate(((1, 1), (1, 2), (2, 1), (2, 2))):
        near(p, q, n == 0)

    def plane(rc, side, first, count):
        rows = pl.ds(2 + first, count)
        own = grid.at[rc, rows, 2:4] if side == 0 else grid.at[rc, rows, nx : nx + 2]
        there = grid.at[rc, rows, nx + 2 : nx + 4] if side == 0 else grid.at[rc, rows, 0:2]
        return pltpu.make_async_remote_copy(
            src_ref=own, dst_ref=there, send_sem=sz_sem.at[rc, side], recv_sem=rz_sem.at[rc, side],
            device_id=(s, d - nx if side == 0 else d + nx), device_id_type=MESH,
        )

    for rc in range(2):
        for step in y_order:
            from_y = lax.rem(y + step, ny)
            for side in range(2):
                part = grid.at[rc, pl.ds(2 + 2 * from_y, 2), 2 + 2 * side : 4 + 2 * side]
                pltpu.make_async_copy(part, part, r1_sem.at[rc, side, from_y]).wait()

                @pl.when(z > 0 if side == 0 else z < nz - 1)
                def _(rc=rc, side=side, from_y=from_y):
                    plane(rc, side, 2 * from_y, 2).start()

        if rc == 0:
            pass_first()
            @pl.when(s != z)
            def _():
                swap.wait_recv()

            turned = trd[...].T
            wide = mix.shape[2]
            lane = lax.broadcasted_iota(jnp.int32, (nq, wide), 1)
            same = lax.rem(lane, nq) == lax.broadcasted_iota(jnp.int32, (nq, wide), 0)
            imag = lax.rem(lane // nq, 2) == 1
            source = jnp.where(same, lane // (2 * nq), -1)
            for row_step in range(-2, 3):
                ks = [(k, b) for k, (a, b) in enumerate(far_offsets) if a == row_step]
                for c in range(2):
                    rows = [jnp.zeros((nq, wide), f32) for _ in range(nx)]
                    for k, b in ks:
                        p, q = (jnp.broadcast_to(turned[0:nq, 2 * k + n : 2 * k + n + 1], (nq, wide)) for n in range(2))
                        value = jnp.where(imag, p, q) if c else jnp.where(imag, -q, p)
                        rows = [jnp.where(source == 2 + col + b, value, rows[col]) for col in range(nx)]
                    for col in range(nx):
                        first = (2 * col + c) * nq
                        mix[row_step + 2, first : first + nq] = rows[col].astype(bf16)

    for rc in range(2):

        @pl.when(z < nz - 1)
        def _(rc=rc):
            plane(rc, 0, 0, ns).wait_recv()

        @pl.when(z > 0)
        def _(rc=rc):
            plane(rc, 1, 0, ns).wait_recv()

        @pl.loop(0, ny)
        def _(i, rc=rc):
            first = 2 * lax.rem(y + lax.rem(lax.shift_right_logical(jnp.int32(y_digits), 2 * i), 4), ny)
            total = jnp.zeros((2 * nx * nq, 2 * LANES), f32)
            for row_step in range(5):
                right = jnp.concatenate(
                    [grid[rc, first + n + row_step].reshape(2 * (nx + 4) * nq, LANES) for n in range(2)], axis=1
                )
                total += dot(mix[row_step], right).astype(bf16).astype(f32)
            for n in range(2):
                inc[rc, pl.ds((first + n) * nx, nx)] = (
                    total[:, n * LANES : (n + 1) * LANES].astype(bf16).reshape(nx, 2, nq, LANES)
                )
            for col in far_columns():
                for n in range(2):
                    t = (first + n) * nx + col
                    src, dst = inc.at[rc, t], back.at[:, dirs_of(me), lanes(rc)]

                    @pl.when(t != me)
                    def _(t=t, src=src):
                        pltpu.make_async_remote_copy(
                            src_ref=src, dst_ref=dst, send_sem=s2_sem.at[rc], recv_sem=r2_sem.at[rc],
                            device_id=owner_device(t), device_id_type=MESH,
                        ).start()

                    @pl.when(t == me)
                    def _(src=src):
                        pltpu.make_async_copy(src, dst, r2_sem.at[rc]).start()

        if rc == 0:
            pass_second()
            columns_came(0)
            start_up((1, 2))
        else:
            columns_came(1)
            start_down((1, 2))

    @pl.when(s < ns - 1)
    def _():
        for copy in up:
            copy.wait_recv()

    @pl.when(s > 0)
    def _():
        for copy in down:
            copy.wait_recv()

    for p in range(4):
        for q in range(4):
            if p in (0, 3) or q in (0, 3):
                near(p, q)

    loads[3].wait()
    for rc in range(2):
        cols = slice(rc * LANES, (rc + 1) * LANES)
        whole = back.at[:, :, cols]
        pltpu.make_async_copy(whole, whole, r2_sem.at[rc]).wait()
        right = stacked(back[0, :, cols], back[1, :, cols])
        for i in range(2):
            left = jnp.concatenate(
                [jnp.concatenate([dis[c, i, j] for c in range(2)], axis=1) for j in range(2)], axis=0
            )
            both = dot(left, right)
            rows = left.shape[0] // 2
            for j in range(2):
                live = live_ref[i, j].astype(f32)
                for c in range(2):
                    part = both[j * rows : (j + 1) * rows, c * LANES : (c + 1) * LANES]
                    acc[c, i, j, :, cols] = (acc[c, i, j, :, cols] + part) * live

    @pl.when(s != z)
    def _():
        swap.wait_send()

    @pl.when(jnp.logical_not(left_end) | after)
    def _():
        to_left(0).wait_send()

    @pl.when(jnp.logical_not(right_end) | before)
    def _():
        to_right(0).wait_send()

    @pl.when(jnp.logical_not(left_end))
    def _():
        to_left(1).wait_send()

    @pl.when(jnp.logical_not(right_end))
    def _():
        to_right(1).wait_send()

    @pl.when(left_end & before | right_end & after)
    def _():
        first_left.wait_send()
        second_left.wait_send()

    @pl.when(right_end & before | left_end & after)
    def _():
        pass_on(3, 1, prev).wait_send()

    @pl.when(s > 0)
    def _():
        for copy in up:
            copy.wait_send()

    @pl.when(s < ns - 1)
    def _():
        for copy in down:
            copy.wait_send()

    for rc in range(2):
        sent = inc.at[rc, 0 : owners - 1]
        pltpu.make_async_copy(sent, sent, s1_sem.at[rc]).wait()
        pltpu.make_async_copy(sent, sent, s2_sem.at[rc]).wait()

        @pl.when(z > 0)
        def _(rc=rc):
            plane(rc, 0, 0, ns).wait_send()

        @pl.when(z < nz - 1)
        def _(rc=rc):
            plane(rc, 1, 0, ns).wait_send()


def shards(ns, nd, unknowns, leaf_live, near_blocks, aggregate, disaggregate, translate):
    nq = translate.shape[2]
    leaf, sides = unknowns.shape[3:]
    dirs = aggregate.shape[3]
    bf16, f32 = jnp.bfloat16, jnp.float32
    owners = ns * PLANE_COLS
    any_space = pl.BlockSpec(memory_space=pl.ANY)
    dma = pltpu.SemaphoreType.DMA
    field = pl.pallas_call(
        functools.partial(kernel, ns, nd),
        out_shape=pltpu.VMEM(unknowns.shape, f32),
        in_specs=[
            pl.BlockSpec(memory_space=pltpu.SMEM),
            any_space,
            any_space,
            any_space,
            any_space,
            pl.BlockSpec(memory_space=pltpu.VMEM),
        ],
        out_specs=pl.BlockSpec(memory_space=pltpu.VMEM),
        scratch_shapes=[
            pltpu.VMEM(unknowns.shape, bf16),
            pltpu.VMEM((4, 4, 2, leaf, sides), bf16),
            pltpu.VMEM((2, 2, leaf, sides), bf16),
            pltpu.VMEM(near_blocks.shape, bf16),
            pltpu.VMEM(aggregate.shape, bf16),
            pltpu.VMEM(disaggregate.shape, bf16),
            pltpu.VMEM((2, dirs, sides), bf16),
            pltpu.VMEM((2, ns + 4, PLANE_COLS + 4, 2, nq, LANES), bf16),
            pltpu.VMEM((2, owners, 2, nq, LANES), bf16),
            pltpu.VMEM((2, dirs, sides), bf16),
            pltpu.VMEM((32, LANES), f32),
            pltpu.VMEM((32, LANES), f32),
            pltpu.VMEM((5, 2 * PLANE_COLS * nq, 2 * (PLANE_COLS + 4) * nq), bf16),
            dma((4,)),
            dma((2, 3)),
            dma((2, 4)),
            dma((2, 6)),
            dma((2, 1)),
            dma((2,)),
            dma((2, 2, ns // 2)),
            dma((2, 2)),
            dma((2, 2)),
            dma((2,)),
            dma((2,)),
        ],
        compiler_params=pltpu.CompilerParams(
            collective_id=0, has_side_effects=True, vmem_limit_bytes=56 * 1024 * 1024
        ),
    )(leaf_live, unknowns, near_blocks, aggregate, disaggregate, translate)
    return field


def solution(mesh):
    in_specs = (
        P(None, "sect", "dir", None, None),
        P("sect", "dir"),
        P(None, "sect", "dir", None, None, None),
        P(None, "sect", "dir", None, None),
        P(None, "sect", "dir", None, None),
        P(None, None, "dir"),
    )
    out_specs = P(None, "sect", "dir", None, None)
    body = functools.partial(shards, mesh.shape["sect"], mesh.shape["dir"])
    return jax.shard_map(body, mesh=mesh, in_specs=in_specs, out_specs=out_specs, check_vma=False)
```

time: 41.8 us -> 33.7 us (0.81)
  Pallas kernels: 39.4 us -> 32.5 us
  local copies, waits for them, and re-layouts: 2.27 us -> 0.97 us
    pallas_call x1, Pallas kernels: 39.4 us -> 32.5 us  [shards(): pl.pallas_call(functools.partial(kernel, ns, nd), out_shape=pltpu.VMEM(un...]
    unnamed x1, local copies, waits for them, and re-layouts: 2.27 us -> 0.97 us
where the time goes in v2:
time: 33.7 us; the launch traced here: 33.5 us
  Pallas kernels  32.5 us (96%)
  local copies, waits for them, and re-layouts  0.97 us (3%)
    pallas_call x1, Pallas kernels, shards(): pl.pallas_call(functools.partial(kernel, ns, nd), out_shape=pltpu.VMEM(un...  32.5 us
    unnamed x1, local copies, waits for them, and re-layouts  0.97 us

profile of v2, /device:TPU:1, one launch (start us, length us, event | category | flops | bytes accessed | tf_op | source)
XLA Modules:
  0.0 33.5 jit_solution(11703234187220962759)
XLA Ops:
  0.0 32.5 %shard_map.64 = f32[2,2,2,128,256]{4,3,2,1,0:T(8,128)S(1)} custom-call(s32[2,2]{1,0:T(2,128)} %live_ref.1, bf16[2,2,2,128,256]{4,3,2,1,0:T(8,128)(2,1)} %unk_hbm.1, bf16[2,2,2,9,128,128]{5,4,3,2,1,0:T(8,128)(2,1)} %nb_hbm.1, bf16[2,2,2,512,128]{4,3,2,1,0:T(8,128)(2,1)} %agg_hbm.1, bf16[2,2,2,128,512]{4,3,2,1,0:T(8,128)(2,1)} %dis_hbm.1, f32[16,2,16]{2,1,0:T(2,128)} %tr_ref.1), custom_call_target="tpu_custom_call" | custom-call | tf_op jit(solution)/shard_map/pallas_call | solution.py:507
  32.5 1.0 %copy.8 = f32[2,2,2,128,256]{4,3,2,1,0:T(8,128)} copy(f32[2,2,2,128,256]{4,3,2,1,0:T(8,128)S(1)} %shard_map.64) | data formatting | bytes 2097152

commit v3 on v2

--- a/solution.py
+++ b/solution.py
@@ -47,21 +47,23 @@
     loads[0].start()
     loads[1].start()
 
-    def owner_device(t):
-        return (t // nx, z * nx + lax.rem(t, nx))
-
     ny = ns // 2
     y, core = s // 2, lax.rem(s, 2)
     y_order = sorted(range(ny), key=lambda step: (-min(step, ny - step), step))
     x_order = sorted(range(nx), key=lambda step: (-min(step, nx - step), step))
     y_digits = sum(step * 4**i for i, step in enumerate(y_order))
-
-    def far_row(i):
-        step = lax.rem(lax.shift_right_logical(jnp.int32(y_digits), 2 * (i // 2)), 4)
-        return lax.rem(y + step, ny) * 2 + lax.rem(core + 1 + lax.rem(i, 2), 2)
-
-    def far_columns():
-        return [lax.rem(x + step, nx) for step in x_order]
+    cores = (1 - core, core)
+
+    def y_at(i):
+        return lax.rem(y + lax.rem(lax.shift_right_logical(jnp.int32(y_digits), 2 * i), 4), ny)
+
+    columns = [lax.rem(x + step, nx) for step in x_order]
+
+    def send(src, dst, row, col, send_sem, recv_sem):
+        pltpu.make_async_remote_copy(
+            src_ref=src, dst_ref=dst, send_sem=send_sem, recv_sem=recv_sem,
+            device_id=(row, z * nx + col), device_id_type=MESH,
+        ).start()
 
     bar = pltpu.get_barrier_semaphore()
 
@@ -113,23 +115,29 @@
                 leaves[1 + i, 1 + j, c] = (raw[c, i, j].astype(f32) * live).astype(bf16)
 
     loads[1].wait()
+    rows = min(256, total_dirs)
     for rc in range(2):
         cols = slice(rc * LANES, (rc + 1) * LANES)
-        right = stacked(
-            *[
-                jnp.concatenate([leaves[1 + i, 1 + j, c, :, cols] for i in range(2) for j in range(2)], axis=0)
-                for c in range(2)
-            ]
-        )
-        rows = min(256, total_dirs)
-        for q0 in range(0, total_dirs, rows):
+
+        @pl.loop(0, total_dirs // rows)
+        def _(n, rc=rc, cols=cols):
+            right = stacked(
+                *[
+                    jnp.concatenate([leaves[1 + i, 1 + j, c, :, cols] for i in range(2) for j in range(2)], axis=0)
+                    for c in range(2)
+                ]
+            )
+            some = pl.ds(pl.multiple_of(n * rows, rows), rows)
             left = jnp.concatenate(
-                [agg[c, i, j, q0 : q0 + rows] for c in range(2) for i in range(2) for j in range(2)], axis=1
+                [agg[c, i, j, some] for c in range(2) for i in range(2) for j in range(2)], axis=1
             )
             both = dot(left, right)
             for c in range(2):
-                pat[c, q0 : q0 + rows, cols] = both[:, c * LANES : (c + 1) * LANES].astype(bf16)
-
+                pat[rc, pl.ds(n * (rows // nq), rows // nq), c] = (
+                    both[:, c * LANES : (c + 1) * LANES].astype(bf16).reshape(rows // nq, nq, LANES)
+                )
+
+    acc[...] = jnp.zeros(acc.shape, f32)
     pl.semaphore_wait(bar, owners - 1 + 2 + jnp.where(s != z, 1, 0))
 
     def remote(src, dst, sems, i, device):
@@ -251,34 +259,18 @@
             for i in which:
                 down[i].start()
 
-    def lanes(rc):
-        return pl.ds(rc * LANES, LANES)
-
-    def dirs_of(t):
-        return pl.ds(pl.multiple_of(t * nq, nq), nq)
-
     start_hops()
 
-    for rc in range(2):
-
-        @pl.loop(0, ns)
-        def _(i, rc=rc):
-            row = far_row(i)
-            for col in far_columns():
-                t = row * nx + col
-                src, dst = pat.at[:, dirs_of(t), lanes(rc)], grid.at[rc, 2 + s, 2 + x]
-                arrived = r1_sem.at[rc, x // 2, y]
-
-                @pl.when(t != me)
-                def _(t=t, src=src):
-                    pltpu.make_async_remote_copy(
-                        src_ref=src, dst_ref=dst, send_sem=s1_sem.at[rc], recv_sem=arrived,
-                        device_id=owner_device(t), device_id_type=MESH,
-                    ).start()
-
-                @pl.when(t == me)
-                def _(src=src):
-                    pltpu.make_async_copy(src, dst, arrived).start()
+    @pl.loop(0, 2)
+    def _(rc):
+        dst, arrived = grid.at[rc, 2 + s, 2 + x], r1_sem.at[rc, x // 2, y]
+        for y_step in y_order:
+            for n, other in enumerate(cores):
+                row = 2 * lax.rem(y + y_step, ny) + other
+                for x_step, col in zip(x_order, columns):
+                    if y_step or x_step or n == 0:
+                        send(pat.at[rc, row * nx + col], dst, row, col, s1_sem.at[rc], arrived)
+        pltpu.make_async_copy(pat.at[rc, me], dst, arrived).start()
 
     start_columns()
     start_up((0,))
@@ -297,9 +289,9 @@
         for rc in range(2):
             clear(grid.at[rc, 2 : ns + 2, nx + 2 : nx + 4])
 
-    def near(p, q, first=False):
+    def near(p, q):
+        targets = [(i, j) for i in range(2) for j in range(2) if 0 <= p - i <= 2 and 0 <= q - j <= 2]
         right = stacked(leaves[p, q, 0], leaves[p, q, 1])
-        targets = [(i, j) for i in range(2) for j in range(2) if 0 <= p - i <= 2 and 0 <= q - j <= 2]
         left = jnp.concatenate(
             [
                 jnp.concatenate([nb[c, i, j, 3 * (p - i) + q - j] for c in range(2)], axis=1)
@@ -312,12 +304,13 @@
         width = both.shape[1] // 2
         for n, (i, j) in enumerate(targets):
             for c in range(2):
-                part = both[n * rows : (n + 1) * rows, c * width : (c + 1) * width]
-                acc[c, i, j] = part if first else acc[c, i, j] + part
+                acc[c, i, j] += both[n * rows : (n + 1) * rows, c * width : (c + 1) * width]
 
     loads[2].wait()
-    for n, (p, q) in enumerate(((1, 1), (1, 2), (2, 1), (2, 2))):
-        near(p, q, n == 0)
+
+    for p in range(1, 3):
+        for q in range(1, 3):
+            near(p, q)
 
     def plane(rc, side, first, count):
         rows = pl.ds(2 + first, count)
@@ -329,8 +322,9 @@
         )
 
     for rc in range(2):
-        for step in y_order:
-            from_y = lax.rem(y + step, ny)
+        @pl.loop(0, ny)
+        def _(i, rc=rc):
+            from_y = y_at(i)
             for side in range(2):
                 part = grid.at[rc, pl.ds(2 + 2 * from_y, 2), 2 + 2 * side : 4 + 2 * side]
                 pltpu.make_async_copy(part, part, r1_sem.at[rc, side, from_y]).wait()
@@ -346,7 +340,7 @@
                 swap.wait_recv()
 
             turned = trd[...].T
-            wide = mix.shape[2]
+            half, wide = mix.shape[1] // 2, mix.shape[2]
             lane = lax.broadcasted_iota(jnp.int32, (nq, wide), 1)
             same = lax.rem(lane, nq) == lax.broadcasted_iota(jnp.int32, (nq, wide), 0)
             imag = lax.rem(lane // nq, 2) == 1
@@ -361,7 +355,10 @@
                         rows = [jnp.where(source == 2 + col + b, value, rows[col]) for col in range(nx)]
                     for col in range(nx):
                         first = (2 * col + c) * nq
-                        mix[row_step + 2, first : first + nq] = rows[col].astype(bf16)
+                        high = rows[col].astype(bf16)
+                        mix[row_step + 2, first : first + nq] = high
+                        rest = (rows[col] - high.astype(f32)).astype(bf16)
+                        mix[row_step + 2, half + first : half + first + nq] = rest
 
     for rc in range(2):
 
@@ -375,32 +372,34 @@
 
         @pl.loop(0, ny)
         def _(i, rc=rc):
-            first = 2 * lax.rem(y + lax.rem(lax.shift_right_logical(jnp.int32(y_digits), 2 * i), 4), ny)
+            first = 2 * y_at(i)
             total = jnp.zeros((2 * nx * nq, 2 * LANES), f32)
             for row_step in range(5):
                 right = jnp.concatenate(
                     [grid[rc, first + n + row_step].reshape(2 * (nx + 4) * nq, LANES) for n in range(2)], axis=1
                 )
-                total += dot(mix[row_step], right).astype(bf16).astype(f32)
+                term = dot(mix[row_step], right)
+                total += (term[: 2 * nx * nq] + term[2 * nx * nq :]).astype(bf16).astype(f32)
             for n in range(2):
                 inc[rc, pl.ds((first + n) * nx, nx)] = (
                     total[:, n * LANES : (n + 1) * LANES].astype(bf16).reshape(nx, 2, nq, LANES)
                 )
-            for col in far_columns():
-                for n in range(2):
-                    t = (first + n) * nx + col
-                    src, dst = inc.at[rc, t], back.at[:, dirs_of(me), lanes(rc)]
-
-                    @pl.when(t != me)
-                    def _(t=t, src=src):
-                        pltpu.make_async_remote_copy(
-                            src_ref=src, dst_ref=dst, send_sem=s2_sem.at[rc], recv_sem=r2_sem.at[rc],
-                            device_id=owner_device(t), device_id_type=MESH,
-                        ).start()
-
-                    @pl.when(t == me)
-                    def _(src=src):
-                        pltpu.make_async_copy(src, dst, r2_sem.at[rc]).start()
+            dst = back.at[rc, me]
+            for n, other in enumerate(cores):
+                row = first + other
+                for x_step, col in zip(x_order, columns):
+                    src, sems = inc.at[rc, row * nx + col], (s2_sem.at[rc], r2_sem.at[rc])
+                    if n == 0 or x_step:
+                        send(src, dst, row, col, *sems)
+                        continue
+
+                    @pl.when(i < ny - 1)
+                    def _(src=src, row=row, col=col, sems=sems):
+                        send(src, dst, row, col, *sems)
+
+                    @pl.when(i == ny - 1)
+                    def _(src=src, sems=sems):
+                        pltpu.make_async_copy(src, dst, sems[1]).start()
 
         if rc == 0:
             pass_second()
@@ -428,9 +427,9 @@
     loads[3].wait()
     for rc in range(2):
         cols = slice(rc * LANES, (rc + 1) * LANES)
-        whole = back.at[:, :, cols]
+        whole = back.at[rc]
         pltpu.make_async_copy(whole, whole, r2_sem.at[rc]).wait()
-        right = stacked(back[0, :, cols], back[1, :, cols])
+        right = stacked(*[back[rc, :, c].reshape(owners * nq, LANES) for c in range(2)])
         for i in range(2):
             left = jnp.concatenate(
                 [jnp.concatenate([dis[c, i, j] for c in range(2)], axis=1) for j in range(2)], axis=0
@@ -523,13 +522,13 @@
             pltpu.VMEM(near_blocks.shape, bf16),
             pltpu.VMEM(aggregate.shape, bf16),
             pltpu.VMEM(disaggregate.shape, bf16),
-            pltpu.VMEM((2, dirs, sides), bf16),
+            pltpu.VMEM((2, owners, 2, nq, LANES), bf16),
             pltpu.VMEM((2, ns + 4, PLANE_COLS + 4, 2, nq, LANES), bf16),
             pltpu.VMEM((2, owners, 2, nq, LANES), bf16),
-            pltpu.VMEM((2, dirs, sides), bf16),
+            pltpu.VMEM((2, owners, 2, nq, LANES), bf16),
             pltpu.VMEM((32, LANES), f32),
             pltpu.VMEM((32, LANES), f32),
-            pltpu.VMEM((5, 2 * PLANE_COLS * nq, 2 * (PLANE_COLS + 4) * nq), bf16),
+            pltpu.VMEM((5, 4 * PLANE_COLS * nq, 2 * (PLANE_COLS + 4) * nq), bf16),
             dma((4,)),
             dma((2, 3)),
             dma((2, 4)),

time: 33.7 us -> 33.8 us (level)
  no operation moved by 1% of the time
where the time goes in v3:
time: 33.8 us; the launch traced here: 33.7 us
  Pallas kernels  32.7 us (97%)
  local copies, waits for them, and re-layouts  0.97 us (3%)
    pallas_call x1, Pallas kernels, shards(): pl.pallas_call(functools.partial(kernel, ns, nd), out_shape=pltpu.VMEM(un...  32.7 us
    unnamed x1, local copies, waits for them, and re-layouts  0.97 us

profile of v3, /device:TPU:1, one launch (start us, length us, event | category | flops | bytes accessed | tf_op | source)
XLA Modules:
  0.0 33.7 jit_solution(10206490104152073309)
XLA Ops:
  0.0 32.7 %shard_map.64 = f32[2,2,2,128,256]{4,3,2,1,0:T(8,128)S(1)} custom-call(s32[2,2]{1,0:T(2,128)} %live_ref.1, bf16[2,2,2,128,256]{4,3,2,1,0:T(8,128)(2,1)} %unk_hbm.1, bf16[2,2,2,9,128,128]{5,4,3,2,1,0:T(8,128)(2,1)} %nb_hbm.1, bf16[2,2,2,512,128]{4,3,2,1,0:T(8,128)(2,1)} %agg_hbm.1, bf16[2,2,2,128,512]{4,3,2,1,0:T(8,128)(2,1)} %dis_hbm.1, f32[16,2,16]{2,1,0:T(2,128)} %tr_ref.1), custom_call_target="tpu_custom_call" | custom-call | tf_op jit(solution)/shard_map/pallas_call | solution.py:506
  32.7 1.0 %copy.8 = f32[2,2,2,128,256]{4,3,2,1,0:T(8,128)} copy(f32[2,2,2,128,256]{4,3,2,1,0:T(8,128)S(1)} %shard_map.64) | data formatting | bytes 2097152

commit v4 on v3

--- a/solution.py
+++ b/solution.py
@@ -137,7 +137,6 @@
                     both[:, c * LANES : (c + 1) * LANES].astype(bf16).reshape(rows // nq, nq, LANES)
                 )
 
-    acc[...] = jnp.zeros(acc.shape, f32)
     pl.semaphore_wait(bar, owners - 1 + 2 + jnp.where(s != z, 1, 0))
 
     def remote(src, dst, sems, i, device):
@@ -304,7 +303,9 @@
         width = both.shape[1] // 2
         for n, (i, j) in enumerate(targets):
             for c in range(2):
-                acc[c, i, j] += both[n * rows : (n + 1) * rows, c * width : (c + 1) * width]
+                part = both[n * rows : (n + 1) * rows, c * width : (c + 1) * width]
+                part = part * live_ref[i, j].astype(f32)
+                acc[c, i, j] = part if (p, q) == (1, 1) else acc[c, i, j] + part
 
     loads[2].wait()
 
@@ -409,23 +410,13 @@
             columns_came(1)
             start_down((1, 2))
 
-    @pl.when(s < ns - 1)
-    def _():
-        for copy in up:
-            copy.wait_recv()
-
-    @pl.when(s > 0)
-    def _():
-        for copy in down:
-            copy.wait_recv()
-
-    for p in range(4):
-        for q in range(4):
-            if p in (0, 3) or q in (0, 3):
-                near(p, q)
+    for p in range(1, 3):
+        for q in (0, 3):
+            near(p, q)
 
     loads[3].wait()
-    for rc in range(2):
+
+    def far(rc):
         cols = slice(rc * LANES, (rc + 1) * LANES)
         whole = back.at[rc]
         pltpu.make_async_copy(whole, whole, r2_sem.at[rc]).wait()
@@ -440,7 +431,27 @@
                 live = live_ref[i, j].astype(f32)
                 for c in range(2):
                     part = both[j * rows : (j + 1) * rows, c * LANES : (c + 1) * LANES]
-                    acc[c, i, j, :, cols] = (acc[c, i, j, :, cols] + part) * live
+                    acc[c, i, j, :, cols] += part * live
+
+    far(0)
+
+    @pl.when(s < ns - 1)
+    def _():
+        for copy in up:
+            copy.wait_recv()
+
+    for q in range(4):
+        near(3, q)
+
+    @pl.when(s > 0)
+    def _():
+        for copy in down:
+            copy.wait_recv()
+
+    for q in range(4):
+        near(0, q)
+
+    far(1)
 
     @pl.when(s != z)
     def _():

time: 33.8 us -> 33.3 us (0.985)
  Pallas kernels: 32.7 us -> 32.2 us
    pallas_call x1, Pallas kernels: 32.7 us -> 32.2 us  [shards(): pl.pallas_call(functools.partial(kernel, ns, nd), out_shape=pltpu.VMEM(un...]
where the time goes in v4:
time: 33.3 us; the launch traced here: 33.1 us
  Pallas kernels  32.2 us (97%)
  local copies, waits for them, and re-layouts  0.97 us (3%)
    pallas_call x1, Pallas kernels, shards(): pl.pallas_call(functools.partial(kernel, ns, nd), out_shape=pltpu.VMEM(un...  32.2 us
    unnamed x1, local copies, waits for them, and re-layouts  0.97 us

profile of v4, /device:TPU:1, one launch (start us, length us, event | category | flops | bytes accessed | tf_op | source)
XLA Modules:
  0.0 33.1 jit_solution(6012045339129187424)
XLA Ops:
  0.0 32.2 %shard_map.64 = f32[2,2,2,128,256]{4,3,2,1,0:T(8,128)S(1)} custom-call(s32[2,2]{1,0:T(2,128)} %live_ref.1, bf16[2,2,2,128,256]{4,3,2,1,0:T(8,128)(2,1)} %unk_hbm.1, bf16[2,2,2,9,128,128]{5,4,3,2,1,0:T(8,128)(2,1)} %nb_hbm.1, bf16[2,2,2,512,128]{4,3,2,1,0:T(8,128)(2,1)} %agg_hbm.1, bf16[2,2,2,128,512]{4,3,2,1,0:T(8,128)(2,1)} %dis_hbm.1, f32[16,2,16]{2,1,0:T(2,128)} %tr_ref.1), custom_call_target="tpu_custom_call" | custom-call | tf_op jit(solution)/shard_map/pallas_call | solution.py:517
  32.2 1.0 %copy.8 = f32[2,2,2,128,256]{4,3,2,1,0:T(8,128)} copy(f32[2,2,2,128,256]{4,3,2,1,0:T(8,128)S(1)} %shard_map.64) | data formatting | bytes 2097152

commit v5 on v4

--- a/solution.py
+++ b/solution.py
@@ -74,14 +74,15 @@
     def _():
         greet((z, s * nx + x))
 
+    for step in (1, nz - 1):
+        greet((s, lax.rem(z + step, nz) * nx + x))
+
     def hops(step):
         return min(step[0], ny - step[0]) + min(step[2], nx - step[2])
 
     steps = [(a, b, c) for a in range(ny) for b in range(2) for c in range(nx)][1:]
     for a, b, c in sorted(steps, key=lambda step: -hops(step)):
         greet((lax.rem(y + a, ny) * 2 + lax.rem(core + b, 2), z * nx + lax.rem(x + c, nx)))
-    for step in (1, nz - 1):
-        greet((s, lax.rem(z + step, nz) * nx + x))
 
     def clear(ref):
         ref[...] = jnp.zeros(ref.shape, ref.dtype)
@@ -147,14 +148,6 @@
 
     swap = remote(trs, trd, t_sem, 0, (z, s * nx + x))
 
-    @pl.when(s != z)
-    def _():
-        swap.start()
-
-    @pl.when(s == z)
-    def _():
-        trd[...] = trs[...]
-
     left_end, right_end = x == 0, x == nx - 1
     before, after = z > 0, z < nz - 1
     left = (s, z * nx + jnp.where(left_end, nx - 1, x - 1))
@@ -264,12 +257,26 @@
     def _(rc):
         dst, arrived = grid.at[rc, 2 + s, 2 + x], r1_sem.at[rc, x // 2, y]
         for y_step in y_order:
-            for n, other in enumerate(cores):
+            for other in range(2):
                 row = 2 * lax.rem(y + y_step, ny) + other
                 for x_step, col in zip(x_order, columns):
-                    if y_step or x_step or n == 0:
+                    if y_step or x_step:
                         send(pat.at[rc, row * nx + col], dst, row, col, s1_sem.at[rc], arrived)
+                        continue
+
+                    @pl.when(core != other)
+                    def _(row=row, col=col):
+                        send(pat.at[rc, row * nx + col], dst, row, col, s1_sem.at[rc], arrived)
+
         pltpu.make_async_copy(pat.at[rc, me], dst, arrived).start()
+
+    @pl.when(s != z)
+    def _():
+        swap.start()
+
+    @pl.when(s == z)
+    def _():
+        trd[...] = trs[...]
 
     start_columns()
     start_up((0,))

time: 33.3 us -> 33.1 us (level)
  no operation moved by 1% of the time
where the time goes in v5:
time: 33.1 us; the launch traced here: 33 us
  Pallas kernels  32 us (97%)
  local copies, waits for them, and re-layouts  0.97 us (3%)
    pallas_call x1, Pallas kernels, shards(): pl.pallas_call(functools.partial(kernel, ns, nd), out_shape=pltpu.VMEM(un...  32 us
    unnamed x1, local copies, waits for them, and re-layouts  0.97 us

profile of v5, /device:TPU:1, one launch (start us, length us, event | category | flops | bytes accessed | tf_op | source)
XLA Modules:
  0.0 33.0 jit_solution(7135459369555164594)
XLA Ops:
  0.0 32.0 %shard_map.64 = f32[2,2,2,128,256]{4,3,2,1,0:T(8,128)S(1)} custom-call(s32[2,2]{1,0:T(2,128)} %live_ref.1, bf16[2,2,2,128,256]{4,3,2,1,0:T(8,128)(2,1)} %unk_hbm.1, bf16[2,2,2,9,128,128]{5,4,3,2,1,0:T(8,128)(2,1)} %nb_hbm.1, bf16[2,2,2,512,128]{4,3,2,1,0:T(8,128)(2,1)} %agg_hbm.1, bf16[2,2,2,128,512]{4,3,2,1,0:T(8,128)(2,1)} %dis_hbm.1, f32[16,2,16]{2,1,0:T(2,128)} %tr_ref.1), custom_call_target="tpu_custom_call" | custom-call | tf_op jit(solution)/shard_map/pallas_call | solution.py:524
  32.0 1.0 %copy.8 = f32[2,2,2,128,256]{4,3,2,1,0:T(8,128)} copy(f32[2,2,2,128,256]{4,3,2,1,0:T(8,128)S(1)} %shard_map.64) | data formatting | bytes 2097152

commit v6 on v5

--- a/solution.py
+++ b/solution.py
@@ -278,9 +278,9 @@
     def _():
         trd[...] = trs[...]
 
-    start_columns()
     start_up((0,))
     start_down((0,))
+    start_columns()
     for rc in range(2):
         clear(grid.at[rc, 0:2])
         clear(grid.at[rc, ns + 2 : ns + 4])

time: 33.1 us -> 33.1 us (level)
  no operation moved by 1% of the time
where the time goes in v6:
time: 33.1 us; the launch traced here: 33 us
  Pallas kernels  32 us (97%)
  local copies, waits for them, and re-layouts  0.97 us (3%)
    pallas_call x1, Pallas kernels, shards(): pl.pallas_call(functools.partial(kernel, ns, nd), out_shape=pltpu.VMEM(un...  32 us
    unnamed x1, local copies, waits for them, and re-layouts  0.97 us

profile of v6, /device:TPU:1, one launch (start us, length us, event | category | flops | bytes accessed | tf_op | source)
XLA Modules:
  0.0 33.0 jit_solution(11396458658882624997)
XLA Ops:
  0.0 32.0 %shard_map.64 = f32[2,2,2,128,256]{4,3,2,1,0:T(8,128)S(1)} custom-call(s32[2,2]{1,0:T(2,128)} %live_ref.1, bf16[2,2,2,128,256]{4,3,2,1,0:T(8,128)(2,1)} %unk_hbm.1, bf16[2,2,2,9,128,128]{5,4,3,2,1,0:T(8,128)(2,1)} %nb_hbm.1, bf16[2,2,2,512,128]{4,3,2,1,0:T(8,128)(2,1)} %agg_hbm.1, bf16[2,2,2,128,512]{4,3,2,1,0:T(8,128)(2,1)} %dis_hbm.1, f32[16,2,16]{2,1,0:T(2,128)} %tr_ref.1), custom_call_target="tpu_custom_call" | custom-call | tf_op jit(solution)/shard_map/pallas_call | solution.py:524
  32.0 1.0 %copy.8 = f32[2,2,2,128,256]{4,3,2,1,0:T(8,128)} copy(f32[2,2,2,128,256]{4,3,2,1,0:T(8,128)S(1)} %shard_map.64) | data formatting | bytes 2097152
